TPU v7x, 32 devices: a whole 2x2x4 slice. The times are simulated.
32 devices in a mesh: groups: 2 (over y), row: 4 (over z), col: 4 (over x, core).
Axes of the slice: x: 2, y: 2, z: 4, core: 2. Of those that a mesh axis runs over, the one named last changes fastest.
Arguments:
- queries: bfloat16 [4096, 1024], P(('groups', 'row'), 'col'), parts along dimension 0, may hold values from -64 to 64
- keys: bfloat16 [4096, 1024], P(('groups', 'col'), 'row'), parts along dimension 0, may hold values from -6 to 6
- values: bfloat16 [4096, 1024], P(('groups', 'col'), 'row'), parts along dimension 0, may hold values from -6 to 6
- cotangent: bfloat16 [4096, 1024], P(('groups', 'row'), 'col'), parts along dimension 0, may hold values from -6 to 6
- block_lists: int32 [32, 16], P(('groups', 'row')), parts along dimension 0, may hold values from 0 to 15, as said below
- block_counts: int32 [32], P(('groups', 'row')), parts along dimension 0, may hold values from 1 to 16, as said below
Outputs:
- attended: bfloat16 [4096, 1024], P(('groups', 'row'), 'col'), parts along dimension 0
- grad_queries: bfloat16 [4096, 1024], P(('groups', 'row'), 'col'), parts along dimension 0
- grad_keys: bfloat16 [4096, 1024], P(('groups', 'col'), 'row'), parts along dimension 0
- grad_values: bfloat16 [4096, 1024], P(('groups', 'col'), 'row'), parts along dimension 0
There are 2 independent parts, one for each index of `groups`. A program takes and returns all parts, laid end to end along the dimension named above; each array names one. Nothing has to cross between parts.
Inputs may be any that keep to these rules, and one draw needn't show every extreme that they name: `block_lists`: each row lists 16 distinct blocks; its first entry is the query block itself. `block_counts`: some query block has all 16 entries live in every draw.
All inputs are finite; a program needn't handle non-finite values.
Results may differ from a plain program's by a relative error of at most 0.011.
Values may be sent and summed in bfloat16 or wider, within the bound.
No kernel may reach another device: no remote copies, remote signals or barrier semaphores. Data moves between devices by JAX's collectives and lax.ppermute only.
A program may use at most 64 MiB of HBM per device.

v0:
```python
import math
import jax
import jax.numpy as jnp
from jax import lax
from jax.sharding import PartitionSpec as P

D = 1024
HEADS = 16
HEAD = 64
BLK = 128
MAXNB = 16
NEG_FILL = -1e30


def tile_scores(query_tile, key_tile, score_scale):
    query_heads = query_tile.reshape(query_tile.shape[0], HEADS, -1)
    key_heads = key_tile.reshape(key_tile.shape[0], HEADS, -1)
    return (
        jnp.einsum("qhd,khd->hqk", query_heads, key_heads, preferred_element_type=jnp.float32)
        * score_scale
    )


def on_device(queries, keys, values, cotangent, block_lists, block_counts):
    score_scale = 1.0 / math.sqrt(HEAD)
    q_full = lax.all_gather(queries, "col", axis=1, tiled=True)
    k_full, v_full = (
        lax.all_gather(keys, "row", axis=1, tiled=True),
        lax.all_gather(values, "row", axis=1, tiled=True),
    )
    q_rows = q_full.shape[0]
    k_rows = k_full.shape[0]
    q_blocks = q_rows // BLK
    k_blocks = k_rows // BLK
    group_size = min(4, q_blocks)
    span_rows = group_size * BLK
    supers = q_blocks // group_size
    tile_count = supers * k_blocks
    first_key = lax.axis_index("col") * k_blocks
    wanted = first_key + jnp.arange(k_blocks, dtype=jnp.int32)
    live_slots = jnp.arange(MAXNB, dtype=jnp.int32)[None, :] < block_counts[:, None]
    block_hit = jnp.any(
        (block_lists[:, :, None] == wanted[None, None, :]) & live_slots[:, :, None], axis=1
    )
    block_hit = block_hit.reshape(supers, group_size, k_blocks).transpose(0, 2, 1)
    row_mask = jnp.repeat(block_hit, BLK, axis=2)
    tile_any = jnp.any(block_hit, axis=2)

    def tile_parts(step):
        super_at = step // k_blocks
        key_at = step % k_blocks
        query_tile = lax.dynamic_slice_in_dim(q_full, super_at * span_rows, span_rows, 0)
        key_tile = lax.dynamic_slice_in_dim(k_full, key_at * BLK, BLK, 0)
        value_tile = lax.dynamic_slice_in_dim(v_full, key_at * BLK, BLK, 0)
        keep_mask = row_mask[super_at, key_at][None, :, None]
        return (super_at, key_at, query_tile, key_tile, value_tile, keep_mask)

    def unchanged(carry):
        return carry

    def stats_step(step, carry):
        super_at, key_at, query_tile, key_tile, value_tile, keep_mask = tile_parts(step)

        def stats_work(state):
            row_top, row_total = state
            scores = jnp.where(keep_mask, tile_scores(query_tile, key_tile, score_scale), NEG_FILL)
            old_top = lax.dynamic_slice_in_dim(row_top, super_at * span_rows, span_rows, 1)
            old_total = lax.dynamic_slice_in_dim(row_total, super_at * span_rows, span_rows, 1)
            new_top = jnp.maximum(old_top, jnp.max(scores, axis=2))
            exp_terms = jnp.where(keep_mask, jnp.exp(scores - new_top[:, :, None]), 0.0)
            fresh = old_total * jnp.exp(old_top - new_top) + jnp.sum(exp_terms, axis=2)
            return (
                lax.dynamic_update_slice_in_dim(row_top, new_top, super_at * span_rows, 1),
                lax.dynamic_update_slice_in_dim(row_total, fresh, super_at * span_rows, 1),
            )

        return lax.cond(tile_any[super_at, key_at], stats_work, unchanged, carry)

    start_top = jnp.full((HEADS, q_rows), NEG_FILL, jnp.float32)
    start_total = jnp.zeros((HEADS, q_rows), jnp.float32)
    local_top, local_total = lax.fori_loop(0, tile_count, stats_step, (start_top, start_total))
    row_top = lax.pmax(local_top.astype(jnp.bfloat16), "col").astype(local_top.dtype)
    row_total = lax.psum(local_total * jnp.exp(local_top - row_top), "col")

    def tile_weights(scores, super_at, keep_mask):
        top_rows = lax.dynamic_slice_in_dim(row_top, super_at * span_rows, span_rows, 1)
        total_rows = lax.dynamic_slice_in_dim(row_total, super_at * span_rows, span_rows, 1)
        ratio = jnp.exp(scores - top_rows[:, :, None]) / total_rows[:, :, None]
        return jnp.where(keep_mask, ratio, 0.0).astype(jnp.bfloat16)

    def output_step(step, carry):
        super_at, key_at, query_tile, key_tile, value_tile, keep_mask = tile_parts(step)

        def output_work(out_rows):
            scores = jnp.where(keep_mask, tile_scores(query_tile, key_tile, score_scale), NEG_FILL)
            weights = tile_weights(scores, super_at, keep_mask)
            value_heads = value_tile.reshape(BLK, HEADS, -1)
            part = jnp.einsum(
                "hqk,khd->qhd", weights, value_heads, preferred_element_type=jnp.float32
            ).reshape(span_rows, -1)
            current = lax.dynamic_slice_in_dim(out_rows, super_at * span_rows, span_rows, 0)
            return lax.dynamic_update_slice_in_dim(
                out_rows, current + part, super_at * span_rows, 0
            )

        return lax.cond(tile_any[super_at, key_at], output_work, unchanged, carry)

    partial_out = lax.fori_loop(0, tile_count, output_step, jnp.zeros((q_rows, D), jnp.float32))
    out_share = lax.psum_scatter(partial_out, "col", scatter_dimension=1, tiled=True).astype(
        jnp.bfloat16
    )
    grad_full, out_full = (
        lax.all_gather(cotangent, "col", axis=1, tiled=True),
        lax.all_gather(out_share, "col", axis=1, tiled=True),
    )
    delta = jnp.einsum(
        "qhd,qhd->hq",
        grad_full.reshape(q_rows, HEADS, -1),
        out_full.reshape(q_rows, HEADS, -1),
        preferred_element_type=jnp.float32,
    )

    def grad_step(step, carry):
        super_at, key_at, query_tile, key_tile, value_tile, keep_mask = tile_parts(step)

        def grad_work(state):
            query_accum, key_accum, value_accum = state
            scores = jnp.where(keep_mask, tile_scores(query_tile, key_tile, score_scale), NEG_FILL)
            weights = tile_weights(scores, super_at, keep_mask)
            grad_tile = lax.dynamic_slice_in_dim(
                grad_full, super_at * span_rows, span_rows, 0
            ).reshape(span_rows, HEADS, -1)
            value_heads = value_tile.reshape(BLK, HEADS, -1)
            key_heads = key_tile.reshape(BLK, HEADS, -1)
            query_heads = query_tile.reshape(span_rows, HEADS, -1)
            dweights = jnp.einsum(
                "qhd,khd->hqk", grad_tile, value_heads, preferred_element_type=jnp.float32
            )
            delta_rows = lax.dynamic_slice_in_dim(delta, super_at * span_rows, span_rows, 1)
            dscores = (weights.astype(jnp.float32) * (dweights - delta_rows[:, :, None])).astype(
                jnp.bfloat16
            )
            query_part = score_scale * jnp.einsum(
                "hqk,khd->qhd", dscores, key_heads, preferred_element_type=jnp.float32
            )
            key_part = score_scale * jnp.einsum(
                "hqk,qhd->khd", dscores, query_heads, preferred_element_type=jnp.float32
            )
            value_part = jnp.einsum(
                "hqk,qhd->khd", weights, grad_tile, preferred_element_type=jnp.float32
            )
            query_now = lax.dynamic_slice_in_dim(query_accum, super_at * span_rows, span_rows, 0)
            key_now = lax.dynamic_slice_in_dim(key_accum, key_at * BLK, BLK, 0)
            value_now = lax.dynamic_slice_in_dim(value_accum, key_at * BLK, BLK, 0)
            query_accum = lax.dynamic_update_slice_in_dim(
                query_accum, query_now + query_part.reshape(span_rows, -1), super_at * span_rows, 0
            )
            key_accum = lax.dynamic_update_slice_in_dim(
                key_accum, key_now + key_part.reshape(BLK, -1), key_at * BLK, 0
            )
            value_accum = lax.dynamic_update_slice_in_dim(
                value_accum, value_now + value_part.reshape(BLK, -1), key_at * BLK, 0
            )
            return (query_accum, key_accum, value_accum)

        return lax.cond(tile_any[super_at, key_at], grad_work, unchanged, carry)

    start_grads = (
        jnp.zeros((q_rows, D), jnp.float32),
        jnp.zeros((k_rows, D), jnp.float32),
        jnp.zeros((k_rows, D), jnp.float32),
    )
    query_parts, key_parts, value_parts = lax.fori_loop(0, tile_count, grad_step, start_grads)
    grad_queries = lax.psum_scatter(query_parts, "col", scatter_dimension=1, tiled=True).astype(
        jnp.bfloat16
    )
    grad_keys, grad_values = (
        lax.psum_scatter(key_parts, "row", scatter_dimension=1, tiled=True),
        lax.psum_scatter(value_parts, "row", scatter_dimension=1, tiled=True),
    )
    return (
        out_share,
        grad_queries,
        grad_keys.astype(jnp.bfloat16),
        grad_values.astype(jnp.bfloat16),
    )


def solution(mesh):
    return jax.shard_map(
        on_device,
        mesh=mesh,
        in_specs=(
            P(("groups", "row"), "col"),
            P(("groups", "col"), "row"),
            P(("groups", "col"), "row"),
            P(("groups", "row"), "col"),
            P(("groups", "row"), None),
            P(("groups", "row")),
        ),
        out_specs=(
            P(("groups", "row"), "col"),
            P(("groups", "row"), "col"),
            P(("groups", "col"), "row"),
            P(("groups", "col"), "row"),
        ),
        check_vma=False,
    )
```

profile of v0, /device:TPU:0, one launch (start us, length us, event | category | flops | bytes accessed | tf_op | source)
XLA Modules:
  0.0 402.9 jit_solution(14908098541145584658)
XLA Ops:
  7.2 1.8 copy.31
  9.1 1.8 copy.30
  11.0 1.8 copy.33
  13.3 16.3 %all-gather.8.cloned.1.call-done = bf16[512,1024]{0,1:T(8,128)(2,1)} async-done(((bf16[512,256]{0,1:T(8,128)(2,1)}), bf16[512,1024]{0,1:T(8,128)(2,1)}) %all-gather.8.cloned.1.call-update) | async-done | bytes 1048592 | tf_op jit(solution)/shard_map/all_gather | solution.py:26
  29.6 30.1 %all-gather.6.cloned.1.call-done = bf16[512,1024]{0,1:T(8,128)(2,1)} async-done(((bf16[512,256]{0,1:T(8,128)(2,1)}), bf16[512,1024]{0,1:T(8,128)(2,1)}) %all-gather.6.cloned.1.call-update) | async-done | bytes 1048592 | tf_op jit(solution)/shard_map/all_gather | solution.py:28
  59.7 21.9 %while.57 = (s32[]{:T(128)}, f32[16,512]{1,0:T(8,128)S(1)}, f32[16,512]{1,0:T(8,128)S(1)}, pred[1,4]{1,0:T(4,128)(4,1)S(1)}, bf16[512,1024]{0,1:T(8,128)(2,1)}, ...) while((s32[]{:T(128)}, f32[16,512]{1,0:T(8,128)S(1)}, ...), condition=%wide.region_7.8_spmd.clone, body=%wide.region_2.7_spmd.clone.sunk | while | flops 142622736 | bytes 10658168 | solution.py:81
  60.3 4.8 %conditional.9 = ((f32[16,512]{1,0:T(8,128)S(1)}, f32[16,512]{1,0:T(8,128)S(1)})) conditional(s32[]{:T(128)} %bitcast.68, (f32[16,512]{1,0:T(8,128)S(1)}, f32[16,512]{1,0:T(8,128)S(1)}) %tuple.194, (pred[4,4]{1,0:T(4,128)(4,1)S(1)}, s32[]{:T(128)}, s32[]{:T(128)}, bf16[512,1024]{0,1:T(8,128)(2,1)}, bf16[512,1024]{0,1:T(8,128)(2,1)}, ...), branch_computations={%region_3.3_spmd, %region_4.6_spmd} | conditional | flops 142622720 | bytes 10657886 | solution.py:77
  62.1 2.0 bitcast_reduce_fusion
  65.8 4.9 %conditional.9 = ((f32[16,512]{1,0:T(8,128)S(1)}, f32[16,512]{1,0:T(8,128)S(1)})) conditional(s32[]{:T(128)} %bitcast.68, (f32[16,512]{1,0:T(8,128)S(1)}, f32[16,512]{1,0:T(8,128)S(1)}) %tuple.194, (pred[4,4]{1,0:T(4,128)(4,1)S(1)}, s32[]{:T(128)}, s32[]{:T(128)}, bf16[512,1024]{0,1:T(8,128)(2,1)}, bf16[512,1024]{0,1:T(8,128)(2,1)}, ...), branch_computations={%region_3.3_spmd, %region_4.6_spmd} | conditional | flops 142622720 | bytes 10657886 | solution.py:77
  67.5 2.0 bitcast_reduce_fusion
  71.3 4.8 %conditional.9 = ((f32[16,512]{1,0:T(8,128)S(1)}, f32[16,512]{1,0:T(8,128)S(1)})) conditional(s32[]{:T(128)} %bitcast.68, (f32[16,512]{1,0:T(8,128)S(1)}, f32[16,512]{1,0:T(8,128)S(1)}) %tuple.194, (pred[4,4]{1,0:T(4,128)(4,1)S(1)}, s32[]{:T(128)}, s32[]{:T(128)}, bf16[512,1024]{0,1:T(8,128)(2,1)}, bf16[512,1024]{0,1:T(8,128)(2,1)}, ...), branch_computations={%region_3.3_spmd, %region_4.6_spmd} | conditional | flops 142622720 | bytes 10657886 | solution.py:77
  73.0 2.0 bitcast_reduce_fusion
  76.8 4.8 %conditional.9 = ((f32[16,512]{1,0:T(8,128)S(1)}, f32[16,512]{1,0:T(8,128)S(1)})) conditional(s32[]{:T(128)} %bitcast.68, (f32[16,512]{1,0:T(8,128)S(1)}, f32[16,512]{1,0:T(8,128)S(1)}) %tuple.194, (pred[4,4]{1,0:T(4,128)(4,1)S(1)}, s32[]{:T(128)}, s32[]{:T(128)}, bf16[512,1024]{0,1:T(8,128)(2,1)}, bf16[512,1024]{0,1:T(8,128)(2,1)}, ...), branch_computations={%region_3.3_spmd, %region_4.6_spmd} | conditional | flops 142622720 | bytes 10657886 | solution.py:77
  78.5 2.0 bitcast_reduce_fusion
  81.6 11.3 %pmax.7 = bf16[16,512]{1,0:T(8,128)(2,1)S(1)} all-reduce(bf16[16,512]{1,0:T(8,128)(2,1)S(1)} %convert_element_type.89), channel_id=1, replica_groups=mesh['groups'=2,'row'=4,'col'=4] {'col'}, use_global_device_ids=true, to_apply=%region_8.9 | all-reduce | flops 8192 | bytes 32768 | tf_op jit(solution)/shard_map/pmax | solution.py:82
  92.9 10.3 %psum.7 = f32[16,512]{1,0:T(8,128)S(1)} all-reduce(f32[16,512]{1,0:T(8,128)S(1)} %exponential_multiply_fusion), channel_id=1, replica_groups=mesh['groups'=2,'row'=4,'col'=4] {'col'}, use_global_device_ids=true, to_apply=%region_9.10 | all-reduce | flops 8192 | bytes 65536 | tf_op jit(solution)/shard_map/psum | solution.py:83
  103.5 36.9 %while.58 = (s32[]{:T(128)}, f32[512,1024]{0,1:T(8,128)S(1)}, pred[1,4]{1,0:T(4,128)(4,1)S(1)}, bf16[512,1024]{0,1:T(8,128)(2,1)}, bf16[512,1024]{0,1:T(8,128)(2...) while((s32[]{:T(128)}, f32[512,1024]{0,1:T(8,128)S(1)}, ...), condition=%wide.region_13.14_spmd.clone, body=%wide.region_10.13_spmd.clone.sunk | while | flops 275251200 | bytes 11083640 | solution.py:108
  104.2 8.6 %conditional.10 = (f32[512,1024]{0,1:T(8,128)S(1)}) conditional(s32[]{:T(128)} %bitcast.69, f32[512,1024]{0,1:T(8,128)S(1)} %get-tuple-element.1617, (pred[4,4]{1,0:T(4,128)(4,1)S(1)}, s32[]{:T(128)}, s32[]{:T(128)}, bf16[512,1024]{0,1:T(8,128)(2,1)}, bf16[512,1024]{0,1:T(8,128)(2,1)S(1)}, /*index=5*/f32[16,512]{1,0:T(8,128)S(1)}, ...), branch_computations={%region_11.11_spmd, %region_12.12_spmd} | conditional | flops 275251200 | bytes 11083342 | solution.py:106
  105.0 1.8 constant_dynamic-slice_fusion.2
  106.8 3.8 fusion.9
  110.6 2.1 bitcast_add_fusion
  113.4 8.6 %conditional.10 = (f32[512,1024]{0,1:T(8,128)S(1)}) conditional(s32[]{:T(128)} %bitcast.69, f32[512,1024]{0,1:T(8,128)S(1)} %get-tuple-element.1617, (pred[4,4]{1,0:T(4,128)(4,1)S(1)}, s32[]{:T(128)}, s32[]{:T(128)}, bf16[512,1024]{0,1:T(8,128)(2,1)}, bf16[512,1024]{0,1:T(8,128)(2,1)S(1)}, /*index=5*/f32[16,512]{1,0:T(8,128)S(1)}, ...), branch_computations={%region_11.11_spmd, %region_12.12_spmd} | conditional | flops 275251200 | bytes 11083342 | solution.py:106
  114.2 1.8 constant_dynamic-slice_fusion.2
  116.0 3.8 fusion.9
  119.8 2.1 bitcast_add_fusion
  122.6 8.6 %conditional.10 = (f32[512,1024]{0,1:T(8,128)S(1)}) conditional(s32[]{:T(128)} %bitcast.69, f32[512,1024]{0,1:T(8,128)S(1)} %get-tuple-element.1617, (pred[4,4]{1,0:T(4,128)(4,1)S(1)}, s32[]{:T(128)}, s32[]{:T(128)}, bf16[512,1024]{0,1:T(8,128)(2,1)}, bf16[512,1024]{0,1:T(8,128)(2,1)S(1)}, /*index=5*/f32[16,512]{1,0:T(8,128)S(1)}, ...), branch_computations={%region_11.11_spmd, %region_12.12_spmd} | conditional | flops 275251200 | bytes 11083342 | solution.py:106
  123.4 1.8 constant_dynamic-slice_fusion.2
  125.2 3.8 fusion.9
  129.1 2.1 bitcast_add_fusion
  131.9 8.6 %conditional.10 = (f32[512,1024]{0,1:T(8,128)S(1)}) conditional(s32[]{:T(128)} %bitcast.69, f32[512,1024]{0,1:T(8,128)S(1)} %get-tuple-element.1617, (pred[4,4]{1,0:T(4,128)(4,1)S(1)}, s32[]{:T(128)}, s32[]{:T(128)}, bf16[512,1024]{0,1:T(8,128)(2,1)}, bf16[512,1024]{0,1:T(8,128)(2,1)S(1)}, /*index=5*/f32[16,512]{1,0:T(8,128)S(1)}, ...), branch_computations={%region_11.11_spmd, %region_12.12_spmd} | conditional | flops 275251200 | bytes 11083342 | solution.py:106
  132.7 1.8 constant_dynamic-slice_fusion.2
  134.4 3.8 fusion.9
  138.3 2.1 bitcast_add_fusion
  142.8 29.6 %reduce-scatter.5.cloned.1.call-done = f32[512,256]{0,1:T(8,128)} async-done(((f32[512,1024]{0,1:T(8,128)}), f32[512,256]{0,1:T(8,128)}) %reduce-scatter.5.cloned.1.call-update) | async-done | bytes 524304 | tf_op jit(solution)/shard_map/reduce_scatter | solution.py:109
  172.3 1.8 convert_element_type.91
  174.2 17.0 %all-gather.12.cloned.1.call-done = bf16[512,1024]{0,1:T(8,128)(2,1)} async-done(((bf16[512,256]{0,1:T(8,128)(2,1)}), bf16[512,1024]{0,1:T(8,128)(2,1)}) %all-gather.12.cloned.1.call-update) | async-done | bytes 1048592 | tf_op jit(solution)/shard_map/all_gather | solution.py:113
  191.2 18.8 %all-gather.14.cloned.1.call-done = bf16[512,1024]{0,1:T(8,128)(2,1)} async-done(((bf16[512,256]{0,1:T(8,128)(2,1)}), bf16[512,1024]{0,1:T(8,128)(2,1)}) %all-gather.14.cloned.1.call-update) | async-done | bytes 1048592 | tf_op jit(solution)/shard_map/all_gather | solution.py:114
  210.0 1.9 fusion.13
  211.9 1.6 broadcast.97.clone.2
  213.5 1.6 broadcast.97.clone.1
  215.1 1.6 broadcast.97
  216.6 51.4 %while.59 = (s32[]{:T(128)}, f32[512,1024]{0,1:T(8,128)}, f32[512,1024]{0,1:T(8,128)}, f32[512,1024]{0,1:T(8,128)}, pred[1,4]{1,0:T(4,128)(4,1)S(1)}, /*index=5*...) while((s32[]{:T(128)}, f32[512,1024]{0,1:T(8,128)}, ...), condition=%wide.region_18.19_spmd.clone, body=%wide.region_15.18_spmd.clone.sunk | while | flops 683016192 | bytes 48078884 | solution.py:173
  217.2 12.3 %conditional.11 = ((f32[512,1024]{0,1:T(8,128)}, f32[512,1024]{0,1:T(8,128)}, f32[512,1024]{0,1:T(8,128)})) conditional(s32[]{:T(128)} %bitcast.70, (f32[512,1024]{0,1:T(8,128)}, f32[512,1024]{0,1:T(8,128)}, f32[512,1024]{0,1:T(8,128)}) %tuple.199, (pred[4,4]{1,0:T(4,128)(4,1)S(1)}, s32[]{:T(128)}, s32[]{:T(128)}, bf16[512,1024]{0,1:T(8,128)(2,1)}, ...), branch_computations={%region_16.16_spmd, %region_17.17_spmd} | conditional | flops 683016192 | bytes 48078500 | solution.py:166
  219.9 1.4 select_convert_fusion.1
  227.2 2.3 constant_dynamic-update-slice_fusion
  230.1 12.3 %conditional.11 = ((f32[512,1024]{0,1:T(8,128)}, f32[512,1024]{0,1:T(8,128)}, f32[512,1024]{0,1:T(8,128)})) conditional(s32[]{:T(128)} %bitcast.70, (f32[512,1024]{0,1:T(8,128)}, f32[512,1024]{0,1:T(8,128)}, f32[512,1024]{0,1:T(8,128)}) %tuple.199, (pred[4,4]{1,0:T(4,128)(4,1)S(1)}, s32[]{:T(128)}, s32[]{:T(128)}, bf16[512,1024]{0,1:T(8,128)(2,1)}, ...), branch_computations={%region_16.16_spmd, %region_17.17_spmd} | conditional | flops 683016192 | bytes 48078500 | solution.py:166
  232.7 1.4 select_convert_fusion.1
  240.0 2.4 constant_dynamic-update-slice_fusion
  242.9 12.3 %conditional.11 = ((f32[512,1024]{0,1:T(8,128)}, f32[512,1024]{0,1:T(8,128)}, f32[512,1024]{0,1:T(8,128)})) conditional(s32[]{:T(128)} %bitcast.70, (f32[512,1024]{0,1:T(8,128)}, f32[512,1024]{0,1:T(8,128)}, f32[512,1024]{0,1:T(8,128)}) %tuple.199, (pred[4,4]{1,0:T(4,128)(4,1)S(1)}, s32[]{:T(128)}, s32[]{:T(128)}, bf16[512,1024]{0,1:T(8,128)(2,1)}, ...), branch_computations={%region_16.16_spmd, %region_17.17_spmd} | conditional | flops 683016192 | bytes 48078500 | solution.py:166
  245.6 1.4 select_convert_fusion.1
  252.9 2.3 constant_dynamic-update-slice_fusion
  255.8 12.3 %conditional.11 = ((f32[512,1024]{0,1:T(8,128)}, f32[512,1024]{0,1:T(8,128)}, f32[512,1024]{0,1:T(8,128)})) conditional(s32[]{:T(128)} %bitcast.70, (f32[512,1024]{0,1:T(8,128)}, f32[512,1024]{0,1:T(8,128)}, f32[512,1024]{0,1:T(8,128)}) %tuple.199, (pred[4,4]{1,0:T(4,128)(4,1)S(1)}, s32[]{:T(128)}, s32[]{:T(128)}, bf16[512,1024]{0,1:T(8,128)(2,1)}, ...), branch_computations={%region_16.16_spmd, %region_17.17_spmd} | conditional | flops 683016192 | bytes 48078500 | solution.py:166
  265.7 2.4 constant_dynamic-update-slice_fusion
  268.1 2.9 copy.37
  271.1 1.5 copy-done.4
  272.6 1.8 copy.35
  274.5 1.5 copy-done.6
  276.0 1.8 copy.36
  279.6 35.4 %reduce-scatter.11.cloned.1.call-done = f32[512,256]{1,0:T(8,128)} async-done(((f32[512,1024]{1,0:T(8,128)}), f32[512,256]{1,0:T(8,128)}) %reduce-scatter.11.cloned.1.call-update) | async-done | bytes 524304 | tf_op jit(solution)/shard_map/reduce_scatter | solution.py:179
  315.0 1.8 convert_element_type.94
  316.8 31.5 %reduce-scatter.7.cloned.1.call-done = f32[512,256]{1,0:T(8,128)} async-done(((f32[512,1024]{1,0:T(8,128)}), f32[512,256]{1,0:T(8,128)}) %reduce-scatter.7.cloned.1.call-update) | async-done | bytes 524304 | tf_op jit(solution)/shard_map/reduce_scatter | solution.py:174
  348.3 1.8 convert_element_type.92
  350.1 44.5 %reduce-scatter.9.cloned.1.call-done = f32[512,256]{1,0:T(8,128)} async-done(((f32[512,1024]{1,0:T(8,128)}), f32[512,256]{1,0:T(8,128)}) %reduce-scatter.9.cloned.1.call-update) | async-done | bytes 524304 | tf_op jit(solution)/shard_map/reduce_scatter | solution.py:178
  394.6 1.8 convert_element_type.93
  (160 shorter events, 54.6 us)
Async XLA Ops:
  7.2 5.7 %copy-start.10 = (s32[4]{0:T(128)S(1)}, s32[4]{0:T(128)}, u32[]{:S(2)}) copy-start(s32[4]{0:T(128)} %param.23) | copy-start | bytes 52
  7.2 5.8 %copy-start.9 = (s32[4,16]{1,0:T(4,128)S(1)}, s32[4,16]{1,0:T(4,128)}, u32[]{:S(2)}) copy-start(s32[4,16]{1,0:T(4,128)} %param.22) | copy-start | bytes 772
  7.2 22.4 %all-gather.8.cloned.1.call-start = ((), (), s32[]{:S(2)}) async-start(), calls=%async_computation.5 | async-start | bytes 1310720 | tf_op jit(solution)/shard_map/all_gather | solution.py:26
  9.1 50.7 %all-gather.6.cloned.1.call-start = ((), (), s32[]{:S(2)}) async-start(), calls=%async_computation.4 | async-start | bytes 1310720 | tf_op jit(solution)/shard_map/all_gather | solution.py:28
  10.9 92.3 %all-gather.10.cloned.1.call-start = ((), (), s32[]{:S(2)}) async-start(), calls=%async_computation.6 | async-start | bytes 1310720 | tf_op jit(solution)/shard_map/all_gather | solution.py:29
  12.8 159.5 %reduce-scatter.5.cloned.1.call-start = ((), (), s32[]{:S(2)}) async-start(), calls=%async_computation.7 | async-start | bytes 2621440 | tf_op jit(solution)/shard_map/reduce_scatter | solution.py:109
  81.6 21.9 %copy-start.1 = (bf16[512,1024]{0,1:T(8,128)(2,1)S(1)}, bf16[512,1024]{0,1:T(8,128)(2,1)}, u32[]{:S(2)}) copy-start(bf16[512,1024]{0,1:T(8,128)(2,1)} %get-tuple-element.1707) | copy-start | bytes 3145732
  140.4 1.3 copy-start.5
  140.4 1.4 copy-start.8
  141.8 49.4 %all-gather.12.cloned.1.call-start = ((), (), s32[]{:S(2)}) async-start(), calls=%async_computation.8 | async-start | bytes 1310720 | tf_op jit(solution)/shard_map/all_gather | solution.py:113
  142.7 67.3 %all-gather.14.cloned.1.call-start = ((), (), s32[]{:S(2)}) async-start(), calls=%async_computation.9 | async-start | bytes 1310720 | tf_op jit(solution)/shard_map/all_gather | solution.py:114
  174.1 140.9 %reduce-scatter.11.cloned.1.call-start = ((), (), s32[]{:S(2)}) async-start(), calls=%async_computation.12 | async-start | bytes 2621440 | tf_op jit(solution)/shard_map/reduce_scatter | solution.py:179
  213.5 3.2 copy-start
  223.7 1.6 copy-start.2
  225.8 1.3 copy-start.3
  236.5 1.6 copy-start.2
  238.7 1.3 copy-start.3
  249.4 1.6 copy-start.2
  251.5 1.3 copy-start.3
  262.2 1.6 copy-start.2
  264.4 1.3 copy-start.3
  271.0 1.6 copy-start.4
  271.0 77.3 %reduce-scatter.7.cloned.1.call-start = ((), (), s32[]{:S(2)}) async-start(), calls=%async_computation.10 | async-start | bytes 2621440 | tf_op jit(solution)/shard_map/reduce_scatter | solution.py:174
  274.4 1.6 copy-start.6
  274.4 120.2 %reduce-scatter.9.cloned.1.call-start = ((), (), s32[]{:S(2)}) async-start(), calls=%async_computation.11 | async-start | bytes 2621440 | tf_op jit(solution)/shard_map/reduce_scatter | solution.py:178
  277.8 0.9 copy-start.7
Sparse Core Ops, SparseCore 0:
  10.2 19.4 all-gather.7
  31.7 27.9 all-gather.5
  61.9 27.4 all-gather.9
  141.9 30.3 reduce-scatter.4
  174.4 16.7 all-gather.11
  193.2 16.7 all-gather.13
  271.1 43.8 reduce-scatter.10
  317.6 30.7 reduce-scatter.6
  350.7 43.8 reduce-scatter.8
where the time goes:
time: 405 us; the launch traced here: 403 us
  waiting for transfers between devices  223 us (55%)
  local copies, waits for them, and re-layouts  54.1 us (13%)
  other arithmetic  41 us (10%)
  matrix products  40.2 us (10%)
  blocking collectives  21.5 us (5%)
  between operations  14 us (3%)
  loops' own time  8.27 us (2%)
    reduce_scatter x1, waiting for transfers between devices, on_device(): lax.psum_scatter(key_parts, 'row', scatter_dimension=1, tiled=True)  44.5 us
    reduce_scatter x1, waiting for transfers between devices, on_device(): lax.psum_scatter(value_parts, 'row', scatter_dimension=1, tiled=True)  35.4 us
    reduce_scatter x1, waiting for transfers between devices, on_device(): lax.psum_scatter(query_parts, 'col', scatter_dimension=1, tiled=True)  31.5 us
    all_gather x1, waiting for transfers between devices, on_device(): lax.all_gather(keys, 'row', axis=1, tiled=True)  30.1 us
    reduce_scatter x1, waiting for transfers between devices, on_device(): lax.psum_scatter(partial_out, 'col', scatter_dimension=1, tiled=True)  29.6 us
    all_gather x1, waiting for transfers between devices, on_device(): lax.all_gather(out_share, 'col', axis=1, tiled=True)  18.8 us
    all_gather x1, waiting for transfers between devices, on_device(): lax.all_gather(cotangent, 'col', axis=1, tiled=True)  17 us
    all_gather x1, waiting for transfers between devices, on_device(): q_full = lax.all_gather(queries, 'col', axis=1, tiled=True)  16.3 us
  transfers between devices with their start and end apart: 9, of which 8 were waited for; matrix products, arithmetic and copies ran while one was open for 8% of the time, Pallas kernels for 0%

commit v1 on v0

--- a/solution.py
+++ b/solution.py
@@ -23,7 +23,12 @@
 
 def on_device(queries, keys, values, cotangent, block_lists, block_counts):
     score_scale = 1.0 / math.sqrt(HEAD)
-    q_full = lax.all_gather(queries, "col", axis=1, tiled=True)
+    ring = [queries]
+    for hop in range(3):
+        ring.append(lax.ppermute(ring[-1], "col", [(dev, (dev + 1) % 4) for dev in range(4)]))
+    q_full = jnp.roll(
+        jnp.concatenate(ring[::-1], axis=1), (lax.axis_index("col") + 1) * ring[0].shape[1], axis=1
+    )
     k_full, v_full = (
         lax.all_gather(keys, "row", axis=1, tiled=True),
         lax.all_gather(values, "row", axis=1, tiled=True),

time: 405 us -> 382 us (0.943)
  waiting for transfers between devices: 223 us -> 205 us
  matrix products: 40.2 us -> 35.3 us
    all_gather x1, waiting for transfers between devices: 30.1 us -> 12.2 us  [on_device(): lax.all_gather(keys, 'row', axis=1, tiled=True)]
    all_gather x1 -> x0, waiting for transfers between devices: 16.3 us -> none  [on_device(): q_full = lax.all_gather(queries, 'col', axis=1, tiled=True)]
    ppermute x0 -> x3, waiting for transfers between devices: none -> 15.3 us  [on_device(): lax.ppermute(ring[-1], 'col', [(dev, (dev + 1) % 4) for dev in range(4)])]
    dot_general x8, matrix products: 13.5 us -> 8.57 us  [tile_scores(): jnp.einsum('qhd,khd->hqk', query_heads, key_heads, preferred_element_type...]
    unnamed x23 -> x28, local copies, waits for them, and re-layouts: 12.4 us -> 11.8 us
  transfers between devices with their start and end apart: 9 -> 11, of which waited for: 8 -> 10; matrix products, arithmetic and copies ran while one was open for 8% -> 7% of each run, Pallas kernels for 0% -> 0%
where the time goes in v1:
time: 382 us; the launch traced here: 381 us
  waiting for transfers between devices  205 us (54%)
  local copies, waits for them, and re-layouts  53.7 us (14%)
  other arithmetic  41.3 us (11%)
  matrix products  35.3 us (9%)
  blocking collectives  21.8 us (6%)
  between operations  14.3 us (4%)
  loops' own time  8.63 us (2%)
    reduce_scatter x1, waiting for transfers between devices, on_device(): lax.psum_scatter(key_parts, 'row', scatter_dimension=1, tiled=True)  44.5 us
    reduce_scatter x1, waiting for transfers between devices, on_device(): lax.psum_scatter(value_parts, 'row', scatter_dimension=1, tiled=True)  35.4 us
    reduce_scatter x1, waiting for transfers between devices, on_device(): lax.psum_scatter(query_parts, 'col', scatter_dimension=1, tiled=True)  31.5 us
    reduce_scatter x1, waiting for transfers between devices, on_device(): lax.psum_scatter(partial_out, 'col', scatter_dimension=1, tiled=True)  29.6 us
    all_gather x1, waiting for transfers between devices, on_device(): lax.all_gather(out_share, 'col', axis=1, tiled=True)  18.8 us
    all_gather x1, waiting for transfers between devices, on_device(): lax.all_gather(cotangent, 'col', axis=1, tiled=True)  17 us
    dot_general x4, matrix products, output_work(): jnp.einsum('hqk,khd->qhd', weights, value_heads, preferred_element_type=j...  15.3 us
    ppermute x3, waiting for transfers between devices, on_device(): lax.ppermute(ring[-1], 'col', [(dev, (dev + 1) % 4) for dev in range(4)])  15.3 us
  transfers between devices with their start and end apart: 11, of which 10 were waited for; matrix products, arithmetic and copies ran while one was open for 7% of the time, Pallas kernels for 0%

profile of v1, /device:TPU:0, one launch (start us, length us, event | category | flops | bytes accessed | tf_op | source)
XLA Modules:
  0.0 380.5 jit_solution(15680987374808511942)
XLA Ops:
  7.2 1.8 copy.34
  10.7 6.0 %collective-permute-done = bf16[512,256]{0,1:T(8,128)(2,1)S(1)} collective-permute-done((bf16[512,256]{0,1:T(8,128)(2,1)S(1)}, bf16[512,256]{0,1:T(8,128)(2,1)S(1)}, u32[]{:S(2)}, u32[]{:S(2)}) %collective-permute-start) | collective-permute-done | bytes 262176 | tf_op jit(solution)/shard_map/ppermute | solution.py:28
  16.7 1.8 copy.39
  18.6 3.9 %collective-permute-done.1 = bf16[512,256]{0,1:T(8,128)(2,1)S(1)} collective-permute-done((bf16[512,256]{0,1:T(8,128)(2,1)S(1)}, bf16[512,256]{0,1:T(8,128)(2,1)S(1)}, u32[]{:S(2)}, u32[]{:S(2)}) %collective-permute-start.1) | collective-permute-done | bytes 262176 | tf_op jit(solution)/shard_map/ppermute | solution.py:28
  22.9 5.4 %collective-permute-done.2 = bf16[512,256]{0,1:T(8,128)(2,1)S(1)} collective-permute-done((bf16[512,256]{0,1:T(8,128)(2,1)S(1)}, bf16[512,256]{0,1:T(8,128)(2,1)S(1)}, u32[]{:S(2)}, u32[]{:S(2)}) %collective-permute-start.2) | collective-permute-done | bytes 262176 | tf_op jit(solution)/shard_map/ppermute | solution.py:28
  28.6 12.2 %all-gather.5.cloned.1.call-done = bf16[512,1024]{0,1:T(8,128)(2,1)} async-done(((bf16[512,256]{0,1:T(8,128)(2,1)}), bf16[512,1024]{0,1:T(8,128)(2,1)}) %all-gather.5.cloned.1.call-update) | async-done | bytes 1048592 | tf_op jit(solution)/shard_map/all_gather | solution.py:33
  40.8 17.3 %while.57 = (s32[]{:T(128)}, f32[16,512]{1,0:T(8,128)S(1)}, f32[16,512]{1,0:T(8,128)S(1)}, pred[1,4]{1,0:T(4,128)(4,1)S(1)}, bf16[512,1024]{0,1:T(8,128)(2,1)}, ...) while((s32[]{:T(128)}, f32[16,512]{1,0:T(8,128)S(1)}, ...), condition=%wide.region_7.8_spmd.clone, body=%wide.region_2.7_spmd.clone.sunk | while | flops 142622736 | bytes 10658168 | solution.py:86
  41.5 3.6 conditional.9
  45.8 3.6 conditional.9
  50.1 3.6 conditional.9
  54.4 3.6 conditional.9
  58.1 11.6 %pmax.7 = bf16[16,512]{1,0:T(8,128)(2,1)S(1)} all-reduce(bf16[16,512]{1,0:T(8,128)(2,1)S(1)} %convert_element_type.89), channel_id=1, replica_groups=mesh['groups'=2,'row'=4,'col'=4] {'col'}, use_global_device_ids=true, to_apply=%region_8.9 | all-reduce | flops 8192 | bytes 32768 | tf_op jit(solution)/shard_map/pmax | solution.py:87
  69.7 10.3 %psum.7 = f32[16,512]{1,0:T(8,128)S(1)} all-reduce(f32[16,512]{1,0:T(8,128)S(1)} %exponential_multiply_fusion), channel_id=1, replica_groups=mesh['groups'=2,'row'=4,'col'=4] {'col'}, use_global_device_ids=true, to_apply=%region_9.10 | all-reduce | flops 8192 | bytes 65536 | tf_op jit(solution)/shard_map/psum | solution.py:88
  80.3 36.9 %while.58 = (s32[]{:T(128)}, f32[512,1024]{0,1:T(8,128)S(1)}, pred[1,4]{1,0:T(4,128)(4,1)S(1)}, bf16[512,1024]{0,1:T(8,128)(2,1)}, bf16[512,1024]{0,1:T(8,128)(2...) while((s32[]{:T(128)}, f32[512,1024]{0,1:T(8,128)S(1)}, ...), condition=%wide.region_13.14_spmd.clone, body=%wide.region_10.13_spmd.clone.sunk | while | flops 275251200 | bytes 11083640 | solution.py:113
  81.0 8.6 %conditional.10 = (f32[512,1024]{0,1:T(8,128)S(1)}) conditional(s32[]{:T(128)} %bitcast.69, f32[512,1024]{0,1:T(8,128)S(1)} %get-tuple-element.1617, (pred[4,4]{1,0:T(4,128)(4,1)S(1)}, s32[]{:T(128)}, s32[]{:T(128)}, bf16[512,1024]{0,1:T(8,128)(2,1)}, bf16[512,1024]{0,1:T(8,128)(2,1)S(1)}, /*index=5*/f32[16,512]{1,0:T(8,128)S(1)}, ...), branch_computations={%region_11.11_spmd, %region_12.12_spmd} | conditional | flops 275251200 | bytes 11083342 | solution.py:111
  81.8 1.8 constant_dynamic-slice_fusion.2
  83.5 3.8 %fusion.9 = f32[16,512,64]{1,2,0:T(8,128)} fusion(bf16[128,16,64]{0,2,1:T(8,128)(2,1)S(1)} %bitcast.81, bf16[128,16,64]{0,2,1:T(8,128)(2,1)} %bitcast.82, bf16[512,16,64]{0,2,1:T(8,128)(2,1)S(1)} %bitcast.72, f32[16,512]{1,0:T(8,128)S(1)} %get-tuple-element.1154, f32[16,512]{1,0:T(8,128)S(1)} %get-tuple-element.1153, ...), kind=kOutput, calls=%fused_computation.15 | convolution fusion | flops 274726912 | bytes 3736064 | tf_op jit(solution)/shard_map/while/body/eval_jaxpr/cond/branch_1_fun/hqk,khd->qhd/dot_general | solution.py:103
  87.4 2.1 bitcast_add_fusion
  90.2 8.6 %conditional.10 = (f32[512,1024]{0,1:T(8,128)S(1)}) conditional(s32[]{:T(128)} %bitcast.69, f32[512,1024]{0,1:T(8,128)S(1)} %get-tuple-element.1617, (pred[4,4]{1,0:T(4,128)(4,1)S(1)}, s32[]{:T(128)}, s32[]{:T(128)}, bf16[512,1024]{0,1:T(8,128)(2,1)}, bf16[512,1024]{0,1:T(8,128)(2,1)S(1)}, /*index=5*/f32[16,512]{1,0:T(8,128)S(1)}, ...), branch_computations={%region_11.11_spmd, %region_12.12_spmd} | conditional | flops 275251200 | bytes 11083342 | solution.py:111
  91.0 1.8 constant_dynamic-slice_fusion.2
  92.8 3.8 %fusion.9 = f32[16,512,64]{1,2,0:T(8,128)} fusion(bf16[128,16,64]{0,2,1:T(8,128)(2,1)S(1)} %bitcast.81, bf16[128,16,64]{0,2,1:T(8,128)(2,1)} %bitcast.82, bf16[512,16,64]{0,2,1:T(8,128)(2,1)S(1)} %bitcast.72, f32[16,512]{1,0:T(8,128)S(1)} %get-tuple-element.1154, f32[16,512]{1,0:T(8,128)S(1)} %get-tuple-element.1153, ...), kind=kOutput, calls=%fused_computation.15 | convolution fusion | flops 274726912 | bytes 3736064 | tf_op jit(solution)/shard_map/while/body/eval_jaxpr/cond/branch_1_fun/hqk,khd->qhd/dot_general | solution.py:103
  96.6 2.1 bitcast_add_fusion
  99.4 8.6 %conditional.10 = (f32[512,1024]{0,1:T(8,128)S(1)}) conditional(s32[]{:T(128)} %bitcast.69, f32[512,1024]{0,1:T(8,128)S(1)} %get-tuple-element.1617, (pred[4,4]{1,0:T(4,128)(4,1)S(1)}, s32[]{:T(128)}, s32[]{:T(128)}, bf16[512,1024]{0,1:T(8,128)(2,1)}, bf16[512,1024]{0,1:T(8,128)(2,1)S(1)}, /*index=5*/f32[16,512]{1,0:T(8,128)S(1)}, ...), branch_computations={%region_11.11_spmd, %region_12.12_spmd} | conditional | flops 275251200 | bytes 11083342 | solution.py:111
  100.2 1.8 constant_dynamic-slice_fusion.2
  102.0 3.8 %fusion.9 = f32[16,512,64]{1,2,0:T(8,128)} fusion(bf16[128,16,64]{0,2,1:T(8,128)(2,1)S(1)} %bitcast.81, bf16[128,16,64]{0,2,1:T(8,128)(2,1)} %bitcast.82, bf16[512,16,64]{0,2,1:T(8,128)(2,1)S(1)} %bitcast.72, f32[16,512]{1,0:T(8,128)S(1)} %get-tuple-element.1154, f32[16,512]{1,0:T(8,128)S(1)} %get-tuple-element.1153, ...), kind=kOutput, calls=%fused_computation.15 | convolution fusion | flops 274726912 | bytes 3736064 | tf_op jit(solution)/shard_map/while/body/eval_jaxpr/cond/branch_1_fun/hqk,khd->qhd/dot_general | solution.py:103
  105.8 2.1 bitcast_add_fusion
  108.6 8.6 %conditional.10 = (f32[512,1024]{0,1:T(8,128)S(1)}) conditional(s32[]{:T(128)} %bitcast.69, f32[512,1024]{0,1:T(8,128)S(1)} %get-tuple-element.1617, (pred[4,4]{1,0:T(4,128)(4,1)S(1)}, s32[]{:T(128)}, s32[]{:T(128)}, bf16[512,1024]{0,1:T(8,128)(2,1)}, bf16[512,1024]{0,1:T(8,128)(2,1)S(1)}, /*index=5*/f32[16,512]{1,0:T(8,128)S(1)}, ...), branch_computations={%region_11.11_spmd, %region_12.12_spmd} | conditional | flops 275251200 | bytes 11083342 | solution.py:111
  109.4 1.8 constant_dynamic-slice_fusion.2
  111.2 3.8 %fusion.9 = f32[16,512,64]{1,2,0:T(8,128)} fusion(bf16[128,16,64]{0,2,1:T(8,128)(2,1)S(1)} %bitcast.81, bf16[128,16,64]{0,2,1:T(8,128)(2,1)} %bitcast.82, bf16[512,16,64]{0,2,1:T(8,128)(2,1)S(1)} %bitcast.72, f32[16,512]{1,0:T(8,128)S(1)} %get-tuple-element.1154, f32[16,512]{1,0:T(8,128)S(1)} %get-tuple-element.1153, ...), kind=kOutput, calls=%fused_computation.15 | convolution fusion | flops 274726912 | bytes 3736064 | tf_op jit(solution)/shard_map/while/body/eval_jaxpr/cond/branch_1_fun/hqk,khd->qhd/dot_general | solution.py:103
  115.1 2.1 bitcast_add_fusion
  119.5 29.6 %reduce-scatter.5.cloned.1.call-done = f32[512,256]{0,1:T(8,128)} async-done(((f32[512,1024]{0,1:T(8,128)}), f32[512,256]{0,1:T(8,128)}) %reduce-scatter.5.cloned.1.call-update) | async-done | bytes 524304 | tf_op jit(solution)/shard_map/reduce_scatter | solution.py:114
  149.1 1.8 convert_element_type.91
  151.0 17.0 %all-gather.9.cloned.1.call-done = bf16[512,1024]{0,1:T(8,128)(2,1)} async-done(((bf16[512,256]{0,1:T(8,128)(2,1)}), bf16[512,1024]{0,1:T(8,128)(2,1)}) %all-gather.9.cloned.1.call-update) | async-done | bytes 1048592 | tf_op jit(solution)/shard_map/all_gather | solution.py:118
  168.0 18.8 %all-gather.11.cloned.1.call-done = bf16[512,1024]{0,1:T(8,128)(2,1)} async-done(((bf16[512,256]{0,1:T(8,128)(2,1)}), bf16[512,1024]{0,1:T(8,128)(2,1)}) %all-gather.11.cloned.1.call-update) | async-done | bytes 1048592 | tf_op jit(solution)/shard_map/all_gather | solution.py:119
  186.8 1.9 fusion.13
  188.7 1.6 broadcast.98.clone.2
  190.3 1.6 broadcast.98.clone.1
  191.9 1.6 broadcast.98
  193.5 51.9 %while.59 = (s32[]{:T(128)}, f32[512,1024]{0,1:T(8,128)}, f32[512,1024]{0,1:T(8,128)}, f32[512,1024]{0,1:T(8,128)}, pred[1,4]{1,0:T(4,128)(4,1)S(1)}, /*index=5*...) while((s32[]{:T(128)}, f32[512,1024]{0,1:T(8,128)}, ...), condition=%wide.region_18.19_spmd.clone, body=%wide.region_15.18_spmd.clone.sunk | while | flops 683016192 | bytes 48078884 | solution.py:178
  194.1 12.3 %conditional.11 = ((f32[512,1024]{0,1:T(8,128)}, f32[512,1024]{0,1:T(8,128)}, f32[512,1024]{0,1:T(8,128)})) conditional(s32[]{:T(128)} %bitcast.70, (f32[512,1024]{0,1:T(8,128)}, f32[512,1024]{0,1:T(8,128)}, f32[512,1024]{0,1:T(8,128)}) %tuple.199, (pred[4,4]{1,0:T(4,128)(4,1)S(1)}, s32[]{:T(128)}, s32[]{:T(128)}, bf16[512,1024]{0,1:T(8,128)(2,1)}, ...), branch_computations={%region_16.16_spmd, %region_17.17_spmd} | conditional | flops 683016192 | bytes 48078500 | solution.py:171
  196.8 1.4 select_convert_fusion.1
  202.7 1.3 copy-done.2
  204.1 2.3 constant_dynamic-update-slice_fusion
  207.0 12.3 %conditional.11 = ((f32[512,1024]{0,1:T(8,128)}, f32[512,1024]{0,1:T(8,128)}, f32[512,1024]{0,1:T(8,128)})) conditional(s32[]{:T(128)} %bitcast.70, (f32[512,1024]{0,1:T(8,128)}, f32[512,1024]{0,1:T(8,128)}, f32[512,1024]{0,1:T(8,128)}) %tuple.199, (pred[4,4]{1,0:T(4,128)(4,1)S(1)}, s32[]{:T(128)}, s32[]{:T(128)}, bf16[512,1024]{0,1:T(8,128)(2,1)}, ...), branch_computations={%region_16.16_spmd, %region_17.17_spmd} | conditional | flops 683016192 | bytes 48078500 | solution.py:171
  209.7 1.4 select_convert_fusion.1
  215.7 1.3 copy-done.2
  217.0 2.4 constant_dynamic-update-slice_fusion
  220.0 12.3 %conditional.11 = ((f32[512,1024]{0,1:T(8,128)}, f32[512,1024]{0,1:T(8,128)}, f32[512,1024]{0,1:T(8,128)})) conditional(s32[]{:T(128)} %bitcast.70, (f32[512,1024]{0,1:T(8,128)}, f32[512,1024]{0,1:T(8,128)}, f32[512,1024]{0,1:T(8,128)}) %tuple.199, (pred[4,4]{1,0:T(4,128)(4,1)S(1)}, s32[]{:T(128)}, s32[]{:T(128)}, bf16[512,1024]{0,1:T(8,128)(2,1)}, ...), branch_computations={%region_16.16_spmd, %region_17.17_spmd} | conditional | flops 683016192 | bytes 48078500 | solution.py:171
  222.7 1.4 select_convert_fusion.1
  230.0 2.3 constant_dynamic-update-slice_fusion
  233.0 12.3 %conditional.11 = ((f32[512,1024]{0,1:T(8,128)}, f32[512,1024]{0,1:T(8,128)}, f32[512,1024]{0,1:T(8,128)})) conditional(s32[]{:T(128)} %bitcast.70, (f32[512,1024]{0,1:T(8,128)}, f32[512,1024]{0,1:T(8,128)}, f32[512,1024]{0,1:T(8,128)}) %tuple.199, (pred[4,4]{1,0:T(4,128)(4,1)S(1)}, s32[]{:T(128)}, s32[]{:T(128)}, bf16[512,1024]{0,1:T(8,128)(2,1)}, ...), branch_computations={%region_16.16_spmd, %region_17.17_spmd} | conditional | flops 683016192 | bytes 48078500 | solution.py:171
  235.7 1.4 select_convert_fusion.1
  242.9 2.4 constant_dynamic-update-slice_fusion
  245.3 2.9 copy.43
  248.3 1.5 copy-done.3
  249.8 1.8 copy.41
  251.7 1.5 copy-done.5
  253.3 1.8 copy.42
  256.9 35.4 %reduce-scatter.11.cloned.1.call-done = f32[512,256]{1,0:T(8,128)} async-done(((f32[512,1024]{1,0:T(8,128)}), f32[512,256]{1,0:T(8,128)}) %reduce-scatter.11.cloned.1.call-update) | async-done | bytes 524304 | tf_op jit(solution)/shard_map/reduce_scatter | solution.py:184
  292.3 1.8 convert_element_type.94
  294.1 31.5 %reduce-scatter.7.cloned.1.call-done = f32[512,256]{1,0:T(8,128)} async-done(((f32[512,1024]{1,0:T(8,128)}), f32[512,256]{1,0:T(8,128)}) %reduce-scatter.7.cloned.1.call-update) | async-done | bytes 524304 | tf_op jit(solution)/shard_map/reduce_scatter | solution.py:179
  325.6 1.8 convert_element_type.92
  327.4 44.5 %reduce-scatter.9.cloned.1.call-done = f32[512,256]{1,0:T(8,128)} async-done(((f32[512,1024]{1,0:T(8,128)}), f32[512,256]{1,0:T(8,128)}) %reduce-scatter.9.cloned.1.call-update) | async-done | bytes 524304 | tf_op jit(solution)/shard_map/reduce_scatter | solution.py:183
  371.9 1.8 convert_element_type.93
  (170 shorter events, 55.9 us)
Async XLA Ops:
  7.2 15.3 %copy-start.9 = (s32[4]{0:T(128)S(1)}, s32[4]{0:T(128)}, u32[]{:S(2)}) copy-start(s32[4]{0:T(128)} %param.23) | copy-start | bytes 52
  7.2 15.4 %copy-start.8 = (s32[4,16]{1,0:T(4,128)S(1)}, s32[4,16]{1,0:T(4,128)}, u32[]{:S(2)}) copy-start(s32[4,16]{1,0:T(4,128)} %param.22) | copy-start | bytes 772
  7.2 33.6 %all-gather.5.cloned.1.call-start = ((), (), s32[]{:S(2)}) async-start(), calls=%async_computation.4 | async-start | bytes 1310720 | tf_op jit(solution)/shard_map/all_gather | solution.py:33
  9.1 71.0 %all-gather.7.cloned.1.call-start = ((), (), s32[]{:S(2)}) async-start(), calls=%async_computation.5 | async-start | bytes 1310720 | tf_op jit(solution)/shard_map/all_gather | solution.py:34
  10.2 6.5 %collective-permute-start = (bf16[512,256]{0,1:T(8,128)(2,1)S(1)}, bf16[512,256]{0,1:T(8,128)(2,1)S(1)}, u32[]{:S(2)}, u32[]{:S(2)}) collective-permute-start(bf16[512,256]{0,1:T(8,128)(2,1)S(1)} %copy.35), channel_id=1, source_target_pairs={{0,1},{1,2},{2,3},{3,0},{4,5},{5,6},{6,7},{7,4},{8,9},{9,10},{10,1... | collective-permute-start | bytes 786440 | tf_op jit(solution)/shard_map/ppermute | solution.py:28
  16.7 5.8 %collective-permute-start.1 = (bf16[512,256]{0,1:T(8,128)(2,1)S(1)}, bf16[512,256]{0,1:T(8,128)(2,1)S(1)}, u32[]{:S(2)}, u32[]{:S(2)}) collective-permute-start(bf16[512,256]{0,1:T(8,128)(2,1)S(1)} %collective-permute-done), channel_id=1, source_target_pairs={{0,1},{1,2},{2,3},{3,0},{4,5},{5,6},{6,7},{7,4},{8,9},{9,10},{10,1... | collective-permute-start | bytes 786440 | tf_op jit(solution)/shard_map/ppermute | solution.py:28
  18.5 130.6 %reduce-scatter.5.cloned.1.call-start = ((), (), s32[]{:S(2)}) async-start(), calls=%async_computation.6 | async-start | bytes 2621440 | tf_op jit(solution)/shard_map/reduce_scatter | solution.py:114
  22.5 5.8 %collective-permute-start.2 = (bf16[512,256]{0,1:T(8,128)(2,1)S(1)}, bf16[512,256]{0,1:T(8,128)(2,1)S(1)}, u32[]{:S(2)}, u32[]{:S(2)}) collective-permute-start(bf16[512,256]{0,1:T(8,128)(2,1)S(1)} %collective-permute-done.1), channel_id=1, source_target_pairs={{0,1},{1,2},{2,3},{3,0},{4,5},{5,6},{6,7},{7,4},{8,9},{9,10},{10,1... | collective-permute-start | bytes 786440 | tf_op jit(solution)/shard_map/ppermute | solution.py:28
  117.2 1.3 copy-start.4
  117.2 1.4 copy-start.7
  118.6 49.4 %all-gather.9.cloned.1.call-start = ((), (), s32[]{:S(2)}) async-start(), calls=%async_computation.7 | async-start | bytes 1310720 | tf_op jit(solution)/shard_map/all_gather | solution.py:118
  119.5 67.3 %all-gather.11.cloned.1.call-start = ((), (), s32[]{:S(2)}) async-start(), calls=%async_computation.8 | async-start | bytes 1310720 | tf_op jit(solution)/shard_map/all_gather | solution.py:119
  150.9 141.4 %reduce-scatter.11.cloned.1.call-start = ((), (), s32[]{:S(2)}) async-start(), calls=%async_computation.11 | async-start | bytes 2621440 | tf_op jit(solution)/shard_map/reduce_scatter | solution.py:184
  190.3 3.2 copy-start
  200.6 1.6 copy-start.1
  202.7 1.3 copy-start.2
  213.6 1.6 copy-start.1
  215.7 1.3 copy-start.2
  226.5 1.6 copy-start.1
  228.7 1.3 copy-start.2
  239.5 1.6 copy-start.1
  241.6 1.3 copy-start.2
  248.2 1.6 copy-start.3
  248.3 77.3 %reduce-scatter.7.cloned.1.call-start = ((), (), s32[]{:S(2)}) async-start(), calls=%async_computation.9 | async-start | bytes 2621440 | tf_op jit(solution)/shard_map/reduce_scatter | solution.py:179
  251.7 1.6 copy-start.5
  251.7 120.2 %reduce-scatter.9.cloned.1.call-start = ((), (), s32[]{:S(2)}) async-start(), calls=%async_computation.10 | async-start | bytes 2621440 | tf_op jit(solution)/shard_map/reduce_scatter | solution.py:183
  255.1 0.9 copy-start.6
Sparse Core Ops, SparseCore 0:
  10.2 30.6 all-gather.4
  43.0 27.4 all-gather.6
  118.7 30.4 reduce-scatter.4
  151.2 16.7 all-gather.8
  170.0 16.7 all-gather.10
  248.4 43.8 reduce-scatter.10
  294.8 30.7 reduce-scatter.6
  328.0 43.8 reduce-scatter.8
